TPU v7x, 256 devices: a whole 4x4x8 slice. The times are simulated.
256 devices in a mesh: row: 8 (over y, x_lo), col: 32 (over x_hi, z, core).
Axes of the slice: x: 4 (x_hi: 2, x_lo: 2; x = x_hi * 2 + x_lo), y: 4, z: 8, core: 2. Of those that a mesh axis runs over, the one named last changes fastest.
Arguments:
- features: bfloat16 [32768, 768], P(('row', 'col')), may hold values from -6 to 6
- cotangent: bfloat16 [32768, 768], P(('row', 'col')), may hold values from -6 to 6
- w_self: bfloat16 [768, 768], replicated, may hold values from -0.21875 to 0.21875
- w_neigh: bfloat16 [768, 768], replicated, may hold values from -0.21875 to 0.21875
- degree: int32 [32768], P(('row', 'col')), may hold values from 16 to 64
- block_cols: int32 [8, 32, 32, 4], P('row', 'col'), may hold values from 0 to 7, as said below
- block_count: int32 [8, 32, 32], P('row', 'col'), may hold values from 0 to 4, as said below
- blocks: bfloat16 [8, 32, 32, 4, 128, 128], P('row', 'col'), may hold values from 0 to 1, as said below
Outputs:
- output: bfloat16 [32768, 768], P(('row', 'col'))
- grad_features: bfloat16 [32768, 768], P(('row', 'col'))
- grad_w_self: float32 [768, 768], replicated
- grad_w_neigh: float32 [768, 768], replicated
Inputs may be any that keep to these rules, and one draw needn't show every extreme that they name: `block_cols`: within one block row of a tile the 4 block columns are distinct. The live slots of a block row are its first block_count ones. `blocks`: every entry of a slot at or past its block row's live count is zero.
All inputs are finite; a program needn't handle non-finite values.
Results may differ from a plain program's by a relative error of at most 0.015.
Values may be sent and summed in bfloat16 or wider, within the bound.
No kernel may reach another device: no remote copies, remote signals or barrier semaphores. Data moves between devices by JAX's collectives and lax.ppermute only.
A program may use at most 128 MiB of HBM per device.

v0:
```python
import jax
import jax.numpy as jnp
from jax import lax
from jax.sharding import PartitionSpec as P


def silu_slope(hidden):
    sigmoid_value = jax.nn.sigmoid(hidden)
    return sigmoid_value * (1.0 + hidden * (1.0 - sigmoid_value))


def per_device(features, cotangent, w_self, w_neigh, degree, block_cols, block_count, blocks):
    node_rows, feature_width = features.shape
    block_size = blocks.shape[-1]
    block_list = block_cols[0, 0]
    row_loads = block_count[0, 0]
    tile_blocks = blocks[0, 0]
    tile_rows, slot_count = block_list.shape
    source_count = lax.axis_size("row") * node_rows // block_size
    source_iota = jnp.arange(source_count, dtype=jnp.int32)
    slot_iota = jnp.arange(slot_count, dtype=jnp.int32)
    live_slots = slot_iota[None, :] < row_loads[:, None]
    placement = (
        (block_list[:, :, None] == source_iota[None, None, :]) & live_slots[:, :, None]
    ).astype(jnp.bfloat16)
    dense_tile = jnp.einsum(
        "rks,rkab->rasb", placement, tile_blocks, preferred_element_type=jnp.bfloat16
    )
    dense_tile = dense_tile.reshape(tile_rows * block_size, source_count * block_size)
    sources = lax.all_gather(features, "row", axis=0, tiled=True)
    summed = lax.psum_scatter(
        jnp.dot(dense_tile, sources, preferred_element_type=jnp.float32),
        "col",
        scatter_dimension=0,
        tiled=True,
    )
    degree_f = degree.astype(jnp.float32)[:, None]
    aggregate = (summed / degree_f).astype(jnp.bfloat16)
    hidden = jnp.dot(features, w_self, preferred_element_type=jnp.float32) + jnp.dot(
        aggregate, w_neigh, preferred_element_type=jnp.float32
    )
    output = jax.nn.silu(hidden).astype(jnp.bfloat16)
    hidden_grad = (cotangent.astype(jnp.float32) * silu_slope(hidden)).astype(jnp.bfloat16)
    grad_scale = float(node_rows * lax.axis_size("row") * lax.axis_size("col")) ** (-0.5)
    across_rows = (((0,), (0,)), ((), ()))
    term_self = (
        lax.dot_general(features, hidden_grad, across_rows, preferred_element_type=jnp.float32)
        * grad_scale
    )
    term_neigh = (
        lax.dot_general(aggregate, hidden_grad, across_rows, preferred_element_type=jnp.float32)
        * grad_scale
    )
    against_cols = (((1,), (1,)), ((), ()))
    neigh_grad = (
        lax.dot_general(hidden_grad, w_neigh, against_cols, preferred_element_type=jnp.float32)
        / degree_f
    ).astype(jnp.bfloat16)
    targets = lax.all_gather(neigh_grad, "col", axis=0, tiled=True)
    gathered = lax.dot_general(dense_tile, targets, across_rows, preferred_element_type=jnp.float32)
    source_part = lax.psum_scatter(
        gathered.astype(jnp.bfloat16), "row", scatter_dimension=0, tiled=True
    ).astype(jnp.float32)
    grad_features = (
        lax.dot_general(hidden_grad, w_self, against_cols, preferred_element_type=jnp.float32)
        + source_part
    ).astype(jnp.bfloat16)
    grad_w_self, grad_w_neigh = lax.psum((term_self, term_neigh), ("row", "col"))
    return (output, grad_features, grad_w_self, grad_w_neigh)


def solution(mesh):
    placed = (
        P(("row", "col"), None),
        P(("row", "col"), None),
        P(),
        P(),
        P(("row", "col")),
        P("row", "col", None, None),
        P("row", "col", None),
        P("row", "col", None, None, None, None),
    )
    return jax.shard_map(
        per_device,
        mesh=mesh,
        in_specs=placed,
        out_specs=(P(("row", "col"), None), P(("row", "col"), None), P(), P()),
        check_vma=False,
    )
```

profile of v0, /device:TPU:4, one launch (start us, length us, event | category | flops | bytes accessed | tf_op | source)
XLA Modules:
  0.0 674.5 jit_solution(432152945170127482)
XLA Ops:
  7.2 0.0 copy-start
  7.2 0.0 all-gather.3.cloned.1.call-start
  7.2 0.7 all-gather.3.cloned.1.call-update
  7.9 0.0 reduce-scatter.3.cloned.1.call-start
  8.0 0.8 copy.12
  8.7 0.7 iota_compare_fusion.1
  9.5 8.8 %fusion.6 = bf16[32,8,128,128]{3,1,2,0:T(8,128)(2,1)} fusion(bf16[32,4,128,128]{3,2,1,0:T(8,128)(2,1)} %bitcast.34, s32[32,4]{1,0:T(8,128)S(1)} %copy.12, pred[32,4]{1,0:T(8,128)(4,1)S(1)} %iota_compare_fusion.1), kind=kOutput, calls=%fused_computation.6 | convolution fusion | flops 33556480 | bytes 12583552 | tf_op jit(solution)/shard_map/rks,rkab->rasb/dot_general | solution.py:26
  18.2 40.3 %all-gather.3.cloned.1.call-done = bf16[1024,768]{1,0:T(8,128)(2,1)} async-done(((bf16[128,768]{1,0:T(8,128)(2,1)}), bf16[1024,768]{1,0:T(8,128)(2,1)}) %all-gather.3.cloned.1.call-update) | async-done | bytes 1572880 | tf_op jit(solution)/shard_map/all_gather | solution.py:30
  58.5 12.2 %fusion.2 = f32[4096,768]{1,0:T(8,128)} fusion(bf16[1024,768]{1,0:T(8,128)(2,1)} %all-gather.3.cloned.1.call-done, bf16[512,8,8,128]{3,2,1,0:T(8,128)(2,1)} %bitcast.32), kind=kOutput, calls=%fused_computation.2 | convolution fusion | flops 6442450944 | bytes 22544384 | tf_op jit(solution)/shard_map/dot_general | solution.py:32
  70.8 0.0 copy-start.5
  70.8 0.0 copy-start.1
  70.8 0.0 copy-start.2
  70.8 0.0 copy-start.4
  70.8 0.0 reduce-scatter.3.cloned.1.call-update
  70.8 0.0 all-gather.5.cloned.1.call-start
  70.9 0.6 copy-done.5
  71.4 0.6 copy-done.1
  72.1 0.0 copy-done.2
  72.1 0.3 fusion.18
  72.4 169.3 %reduce-scatter.3.cloned.1.call-done = f32[128,768]{1,0:T(8,128)} async-done(((f32[4096,768]{1,0:T(8,128)}), f32[128,768]{1,0:T(8,128)}) %reduce-scatter.3.cloned.1.call-update) | async-done | bytes 393232 | tf_op jit(solution)/shard_map/reduce_scatter | solution.py:31
  241.7 0.0 copy-done
  241.7 0.0 copy-done.4
  241.7 2.1 multiply_convert_fusion
  243.8 0.0 copy-start.3
  243.8 1.2 fusion.12
  245.0 0.0 all-gather.5.cloned.1.call-update
  245.0 0.0 all-reduce.3.cloned.1.call-start
  245.1 1.9 multiply_bitcast_fusion
  247.0 0.0 copy-done.3
  247.0 2.0 convolution_multiply_fusion
  249.0 0.0 all-reduce.3.cloned.1.call-update
  249.0 0.0 reduce-scatter.5.cloned.1.call-start
  249.0 89.1 %all-gather.5.cloned.1.call-done = bf16[4096,768]{1,0:T(8,128)(2,1)} async-done(((bf16[128,768]{1,0:T(8,128)(2,1)}), bf16[4096,768]{1,0:T(8,128)(2,1)}) %all-gather.5.cloned.1.call-update) | async-done | bytes 6291472 | tf_op jit(solution)/shard_map/all_gather | solution.py:59
  338.1 11.7 %fusion.8 = bf16[1024,768]{1,0:T(8,128)(2,1)} fusion(bf16[4096,768]{1,0:T(8,128)(2,1)} %all-gather.5.cloned.1.call-done, bf16[512,8,8,128]{3,2,1,0:T(8,128)(2,1)} %bitcast.33), kind=kOutput, calls=%fused_computation.10 | convolution fusion | flops 6443237376 | bytes 16252928 | tf_op jit(solution)/shard_map/dot_general | solution.py:60
  349.8 0.0 reduce-scatter.5.cloned.1.call-update
  349.8 264.9 %all-reduce.3.cloned.1.call-done = (f32[768,768]{0,1:T(8,128)}, f32[768,768]{1,0:T(8,128)}) async-done(((f32[768,768]{0,1:T(8,128)}, f32[768,768]{1,0:T(8,128)}), (f32[768,768]{0,1:T(8,128)}, f32[768,768]{1,0:T(8,128)})) %all-reduce.3.cloned.1.call-update) | async-done | bytes 4718608 | tf_op jit(solution)/shard_map/psum | solution.py:68
  614.7 3.0 copy.14
  617.8 44.8 %reduce-scatter.5.cloned.1.call-done = bf16[128,768]{1,0:T(8,128)(2,1)} async-done(((bf16[1024,768]{1,0:T(8,128)(2,1)}), bf16[128,768]{1,0:T(8,128)(2,1)}) %reduce-scatter.5.cloned.1.call-update) | async-done | bytes 196624 | tf_op jit(solution)/shard_map/reduce_scatter | solution.py:61
  662.6 2.1 fusion.11
  664.7 3.2 copy.31
  (1 shorter events, 0.0 us)
Async XLA Ops:
  7.2 234.5 %copy-start = (bf16[768,768]{1,0:T(8,128)(2,1)S(1)}, bf16[768,768]{1,0:T(8,128)(2,1)}, u32[]{:S(2)}) copy-start(bf16[768,768]{1,0:T(8,128)(2,1)} %param.11) | copy-start | bytes 3538948
  7.2 51.3 %all-gather.3.cloned.1.call-start = ((), (), s32[]{:S(2)}) async-start(), calls=%async_computation.2 | async-start | bytes 1769472 | tf_op jit(solution)/shard_map/all_gather | solution.py:30
  7.9 233.8 %reduce-scatter.3.cloned.1.call-start = ((), (), s32[]{:S(2)}) async-start(), calls=%async_computation.3 | async-start | bytes 12976128 | tf_op jit(solution)/shard_map/reduce_scatter | solution.py:31
  70.8 0.7 copy-start.5
  70.8 1.3 copy-start.1
  70.8 1.3 copy-start.2
  70.8 170.9 %copy-start.4 = (bf16[128,768]{1,0:T(8,128)(2,1)S(1)}, bf16[128,768]{1,0:T(8,128)(2,1)}, u32[]{:S(2)}) copy-start(bf16[128,768]{1,0:T(8,128)(2,1)} %param.9) | copy-start | bytes 589828
  70.8 267.3 %all-gather.5.cloned.1.call-start = ((), (), s32[]{:S(2)}) async-start(), calls=%async_computation.4 | async-start | bytes 6488064 | tf_op jit(solution)/shard_map/all_gather | solution.py:59
  243.8 3.2 copy-start.3
  245.0 369.7 %all-reduce.3.cloned.1.call-start = ((), (), s32[]{:S(2)}) async-start(), calls=%async_computation.6 | async-start | bytes 9437184 | tf_op jit(solution)/shard_map/psum | solution.py:68
  249.0 413.6 %reduce-scatter.5.cloned.1.call-start = ((), (), s32[]{:S(2)}) async-start(), calls=%async_computation.5 | async-start | bytes 1769472 | tf_op jit(solution)/shard_map/reduce_scatter | solution.py:61
Sparse Core Ops, SparseCore 0:
  9.8 48.6 all-gather.2
  70.9 170.6 reduce-scatter.2
  245.2 92.8 all-gather.4
  344.1 270.5 all-reduce.2
  617.3 45.2 reduce-scatter.4
where the time goes:
time: 675 us; the launch traced here: 674 us
  waiting for transfers between devices  609 us (90%)
  matrix products  42.4 us (6%)
  between operations  13.8 us (2%)
  local copies, waits for them, and re-layouts  8.25 us (1%)
    psum x1, waiting for transfers between devices, per_device(): lax.psum((term_self, term_neigh), ('row', 'col'))  265 us
    reduce_scatter x1, waiting for transfers between devices, per_device(): lax.psum_scatter(jnp.dot(dense_tile, sources, preferred_element_type=jnp....  169 us
    all_gather x1, waiting for transfers between devices, per_device(): targets = lax.all_gather(neigh_grad, 'col', axis=0, tiled=True)  89.1 us
    reduce_scatter x1, waiting for transfers between devices, per_device(): lax.psum_scatter(gathered.astype(jnp.bfloat16), 'row', scatter_dimension=...  44.8 us
    all_gather x1, waiting for transfers between devices, per_device(): sources = lax.all_gather(features, 'row', axis=0, tiled=True)  40.3 us
  transfers between devices with their start and end apart: 5, of which 5 were waited for; matrix products, arithmetic and copies ran while one was open for 4% of the time, Pallas kernels for 0%

commit v1 on v0

--- a/solution.py
+++ b/solution.py
@@ -56,7 +56,9 @@
         lax.dot_general(hidden_grad, w_neigh, against_cols, preferred_element_type=jnp.float32)
         / degree_f
     ).astype(jnp.bfloat16)
-    targets = lax.all_gather(neigh_grad, "col", axis=0, tiled=True)
+    targets = jnp.concatenate(
+        lax.all_to_all(jnp.stack([neigh_grad] * lax.axis_size("col")), "col", 0, 0), axis=0
+    )
     gathered = lax.dot_general(dense_tile, targets, across_rows, preferred_element_type=jnp.float32)
     source_part = lax.psum_scatter(
         gathered.astype(jnp.bfloat16), "row", scatter_dimension=0, tiled=True

time: 675 us -> 651 us (0.964)
  waiting for transfers between devices: 609 us -> 573 us
  starting transfers between devices: 0.2 us -> 9.39 us
    all_to_all x0 -> x1, waiting for transfers between devices: none -> 148 us  [per_device(): lax.all_to_all(jnp.stack([neigh_grad] * lax.axis_size('col')), 'col', 0, 0)]
    psum x1, waiting for transfers between devices: 265 us -> 169 us  [per_device(): lax.psum((term_self, term_neigh), ('row', 'col'))]
    all_gather x1 -> x0, waiting for transfers between devices: 89.1 us -> none  [per_device(): targets = lax.all_gather(neigh_grad, 'col', axis=0, tiled=True)]
    all_to_all x0 -> x1, starting transfers between devices: none -> 9.05 us  [per_device(): lax.all_to_all(jnp.stack([neigh_grad] * lax.axis_size('col')), 'col', 0, 0)]
where the time goes in v1:
time: 651 us; the launch traced here: 650 us
  waiting for transfers between devices  573 us (88%)
  matrix products  41.7 us (6%)
  between operations  13.8 us (2%)
  local copies, waits for them, and re-layouts  11.7 us (2%)
  starting transfers between devices  9.39 us (1%)
    psum x1, waiting for transfers between devices, per_device(): lax.psum((term_self, term_neigh), ('row', 'col'))  169 us
    reduce_scatter x1, waiting for transfers between devices, per_device(): lax.psum_scatter(jnp.dot(dense_tile, sources, preferred_element_type=jnp....  169 us
    all_to_all x1, waiting for transfers between devices, per_device(): lax.all_to_all(jnp.stack([neigh_grad] * lax.axis_size('col')), 'col', 0, 0)  148 us
    reduce_scatter x1, waiting for transfers between devices, per_device(): lax.psum_scatter(gathered.astype(jnp.bfloat16), 'row', scatter_dimension=...  44.9 us
    all_gather x1, waiting for transfers between devices, per_device(): sources = lax.all_gather(features, 'row', axis=0, tiled=True)  40.3 us
  transfers between devices with their start and end apart: 5, of which 5 were waited for; matrix products, arithmetic and copies ran while one was open for 4% of the time, Pallas kernels for 0%

profile of v1, /device:TPU:4, one launch (start us, length us, event | category | flops | bytes accessed | tf_op | source)
XLA Modules:
  0.0 650.2 jit_solution(154391257745947364)
XLA Ops:
  7.2 0.0 copy-start
  7.2 0.0 all-gather.2.cloned.1.call-start
  7.2 0.7 all-gather.2.cloned.1.call-update
  7.9 0.0 reduce-scatter.3.cloned.1.call-start
  8.0 0.8 copy.12
  8.7 0.7 iota_compare_fusion.1
  9.5 8.8 %fusion.6 = bf16[32,8,128,128]{3,1,2,0:T(8,128)(2,1)} fusion(bf16[32,4,128,128]{3,2,1,0:T(8,128)(2,1)} %bitcast.35, s32[32,4]{1,0:T(8,128)S(1)} %copy.12, pred[32,4]{1,0:T(8,128)(4,1)S(1)} %iota_compare_fusion.1), kind=kOutput, calls=%fused_computation.6 | convolution fusion | flops 33556480 | bytes 12583552 | tf_op jit(solution)/shard_map/rks,rkab->rasb/dot_general | solution.py:26
  18.2 40.3 %all-gather.2.cloned.1.call-done = bf16[1024,768]{1,0:T(8,128)(2,1)} async-done(((bf16[128,768]{1,0:T(8,128)(2,1)}), bf16[1024,768]{1,0:T(8,128)(2,1)}) %all-gather.2.cloned.1.call-update) | async-done | bytes 1572880 | tf_op jit(solution)/shard_map/all_gather | solution.py:30
  58.5 12.2 %fusion.2 = f32[4096,768]{1,0:T(8,128)} fusion(bf16[1024,768]{1,0:T(8,128)(2,1)} %all-gather.2.cloned.1.call-done, bf16[512,8,8,128]{3,2,1,0:T(8,128)(2,1)} %bitcast.33), kind=kOutput, calls=%fused_computation.2 | convolution fusion | flops 6442450944 | bytes 22544384 | tf_op jit(solution)/shard_map/dot_general | solution.py:32
  70.8 0.0 copy-start.5
  70.8 0.0 copy-start.1
  70.8 0.0 copy-start.2
  70.8 0.0 copy-start.4
  70.8 0.0 reduce-scatter.3.cloned.1.call-update
  70.8 0.6 copy-done.5
  71.4 0.6 copy-done.1
  72.1 0.0 copy-done.2
  72.1 0.3 fusion.18
  72.4 169.3 %reduce-scatter.3.cloned.1.call-done = f32[128,768]{1,0:T(8,128)} async-done(((f32[4096,768]{1,0:T(8,128)}), f32[128,768]{1,0:T(8,128)}) %reduce-scatter.3.cloned.1.call-update) | async-done | bytes 393232 | tf_op jit(solution)/shard_map/reduce_scatter | solution.py:31
  241.7 0.0 copy-done
  241.7 0.0 copy-done.4
  241.7 2.1 multiply_convert_fusion
  243.9 0.5 fusion.12
  244.4 3.4 stack.2
  247.8 9.1 %all-to-all-start = ((bf16[32,128,768]{2,1,0:T(8,128)(2,1)}), bf16[32,128,768]{2,1,0:T(8,128)(2,1)}, u32[]{:S(2)}, u32[]{:S(2)}) async-start(bf16[32,128,768]{2,1,0:T(8,128)(2,1)} %stack.2), calls=%async_computation.1 | async-start | bytes 12582912 | tf_op jit(solution)/shard_map/all_to_all | solution.py:60
  256.8 0.0 copy-start.3
  256.8 0.0 all-reduce.3.cloned.1.call-start
  256.9 1.9 multiply_bitcast_fusion
  258.8 0.0 copy-done.3
  258.8 2.0 convolution_multiply_fusion
  260.8 0.0 all-reduce.3.cloned.1.call-update
  260.8 0.2 reduce-scatter.5.cloned.1.call-start
  261.0 148.3 %all-to-all-done = bf16[32,128,768]{2,1,0:T(8,128)(2,1)} async-done(((bf16[32,128,768]{2,1,0:T(8,128)(2,1)}), bf16[32,128,768]{2,1,0:T(8,128)(2,1)}, u32[]{:S(2)}, u32[]{:S(2)}) %all-to-all-start) | async-done | bytes 6291488 | tf_op jit(solution)/shard_map/all_to_all | solution.py:60
  409.3 11.7 %fusion.8 = bf16[1024,768]{1,0:T(8,128)(2,1)} fusion(bf16[4096,768]{1,0:T(8,128)(2,1)} %bitcast.6, bf16[512,8,8,128]{3,2,1,0:T(8,128)(2,1)} %bitcast.34), kind=kOutput, calls=%fused_computation.10 | convolution fusion | flops 6443237376 | bytes 16252928 | tf_op jit(solution)/shard_map/dot_general | solution.py:62
  421.0 0.0 reduce-scatter.5.cloned.1.call-update
  421.0 169.4 %all-reduce.3.cloned.1.call-done = (f32[768,768]{0,1:T(8,128)}, f32[768,768]{1,0:T(8,128)}) async-done(((f32[768,768]{0,1:T(8,128)}, f32[768,768]{1,0:T(8,128)}), (f32[768,768]{0,1:T(8,128)}, f32[768,768]{1,0:T(8,128)})) %all-reduce.3.cloned.1.call-update) | async-done | bytes 4718608 | tf_op jit(solution)/shard_map/psum | solution.py:70
  590.4 3.0 copy.14
  593.5 44.9 %reduce-scatter.5.cloned.1.call-done = bf16[128,768]{1,0:T(8,128)(2,1)} async-done(((bf16[1024,768]{1,0:T(8,128)(2,1)}), bf16[128,768]{1,0:T(8,128)(2,1)}) %reduce-scatter.5.cloned.1.call-update) | async-done | bytes 196624 | tf_op jit(solution)/shard_map/reduce_scatter | solution.py:63
  638.3 2.1 fusion.11
  640.5 3.2 copy.31
  (1 shorter events, 0.0 us)
Async XLA Ops:
  7.2 234.6 %copy-start = (bf16[768,768]{1,0:T(8,128)(2,1)S(1)}, bf16[768,768]{1,0:T(8,128)(2,1)}, u32[]{:S(2)}) copy-start(bf16[768,768]{1,0:T(8,128)(2,1)} %param.11) | copy-start | bytes 3538948
  7.2 51.3 %all-gather.2.cloned.1.call-start = ((), (), s32[]{:S(2)}) async-start(), calls=%async_computation.3 | async-start | bytes 1769472 | tf_op jit(solution)/shard_map/all_gather | solution.py:30
  7.9 233.8 %reduce-scatter.3.cloned.1.call-start = ((), (), s32[]{:S(2)}) async-start(), calls=%async_computation.4 | async-start | bytes 12976128 | tf_op jit(solution)/shard_map/reduce_scatter | solution.py:31
  70.8 0.7 copy-start.5
  70.8 1.3 copy-start.1
  70.8 1.3 copy-start.2
  70.8 171.0 %copy-start.4 = (bf16[128,768]{1,0:T(8,128)(2,1)S(1)}, bf16[128,768]{1,0:T(8,128)(2,1)}, u32[]{:S(2)}) copy-start(bf16[128,768]{1,0:T(8,128)(2,1)} %param.9) | copy-start | bytes 589828
  247.8 161.6 %all-to-all-start = ((bf16[32,128,768]{2,1,0:T(8,128)(2,1)}), bf16[32,128,768]{2,1,0:T(8,128)(2,1)}, u32[]{:S(2)}, u32[]{:S(2)}) async-start(bf16[32,128,768]{2,1,0:T(8,128)(2,1)} %stack.2), calls=%async_computation.1 | async-start | bytes 12582912 | tf_op jit(solution)/shard_map/all_to_all | solution.py:60
  256.8 2.0 copy-start.3
  256.8 333.6 %all-reduce.3.cloned.1.call-start = ((), (), s32[]{:S(2)}) async-start(), calls=%async_computation.6 | async-start | bytes 9437184 | tf_op jit(solution)/shard_map/psum | solution.py:70
  260.8 377.5 %reduce-scatter.5.cloned.1.call-start = ((), (), s32[]{:S(2)}) async-start(), calls=%async_computation.5 | async-start | bytes 1769472 | tf_op jit(solution)/shard_map/reduce_scatter | solution.py:63
Sparse Core Ops, SparseCore 0:
  9.8 48.6 all-gather.1
  70.9 170.7 reduce-scatter.2
  263.8 326.5 all-reduce.2
  593.0 45.2 reduce-scatter.4
